TPU v7x, 32 devices: a whole 2x2x4 slice. The times are simulated.
32 devices in a mesh: grp: 2 (over y), row: 4 (over x, core), col: 4 (over z).
Axes of the slice: x: 2, y: 2, z: 4, core: 2. Of those that a mesh axis runs over, the one named last changes fastest.
Arguments:
- programs: bfloat16 [2048, 2048], P(('grp', 'row'), 'col'), parts along dimension 0, may hold values from -6 to 6
- tests: bfloat16 [2048, 2048], P(('grp', 'col'), 'row'), parts along dimension 0, may hold values from -6 to 6
- weight: bfloat16 [2048, 2048], P('col', 'row'), may hold values from -0.125 to 0.125
- labels: int32 [2048, 1024], P(('grp', 'row'), 'col'), parts along dimension 0, may hold values 0 or 1
Outputs:
- grad_programs: bfloat16 [2048, 2048], P(('grp', 'row'), 'col'), parts along dimension 0
- grad_tests: bfloat16 [2048, 2048], P(('grp', 'col'), 'row'), parts along dimension 0
- grad_weight: float32 [4096, 2048], P(('grp', 'col'), 'row'), parts along dimension 0
There are 2 independent parts, one for each index of `grp`. A program takes and returns all parts, laid end to end along the dimension named above; an argument that names none is the same for every part. Nothing has to cross between parts.
All inputs are finite; a program needn't handle non-finite values. No bound on the sum of `labels` on one device may be relied on, other than what follows from the above.
Results may differ from a plain program's by a relative error of at most 0.017.
Values may be sent and summed in bfloat16 or wider, within the bound.
A program may use at most 64 MiB of HBM per device.

v0:
```python
import math
import jax
import jax.numpy as jnp
from jax import lax
from jax.sharding import PartitionSpec as P

E = 2048


def contract(left, right, left_dim, right_dim):
    return lax.dot_general(
        left, right, (((left_dim,), (right_dim,)), ((), ())), preferred_element_type=jnp.float32
    )


def local(programs, tests, weight, labels):
    factor = 1.0 / math.sqrt(E)
    targets = labels.astype(jnp.float32)
    w_rows = lax.all_gather(weight, "row", axis=1, tiled=True)
    share = lax.psum_scatter(
        jnp.dot(programs, w_rows, preferred_element_type=jnp.float32).astype(jnp.bfloat16),
        "col",
        scatter_dimension=0,
        tiled=True,
    )
    projected = lax.all_gather(share, "col", axis=0, tiled=True)
    test_whole = lax.all_gather(tests, "row", axis=1, tiled=True)
    logits = contract(projected, test_whole, 1, 1) * factor
    dlogits = (jax.nn.sigmoid(logits) - targets).astype(jnp.bfloat16)
    partial_sums = jnp.dot(dlogits, test_whole, preferred_element_type=jnp.float32)
    summed = lax.psum(partial_sums.astype(jnp.bfloat16), "col")
    grad_programs = (contract(summed, w_rows, 1, 1) * factor).astype(jnp.bfloat16)
    weight_part = contract(programs, summed, 0, 0) * factor
    test_part = contract(dlogits, projected, 0, 0) * factor
    grad_weight, test_total = (
        lax.psum_scatter(
            weight_part.astype(jnp.bfloat16), "row", scatter_dimension=1, tiled=True
        ).astype(jnp.float32),
        lax.psum_scatter(
            test_part.astype(jnp.bfloat16), "row", scatter_dimension=1, tiled=True
        ).astype(jnp.float32),
    )
    grad_tests = test_total.astype(jnp.bfloat16)
    return (grad_programs, grad_tests, grad_weight)


def solution(mesh):
    placed = (
        P(("grp", "row"), "col"),
        P(("grp", "col"), "row"),
        P("col", "row"),
        P(("grp", "row"), "col"),
    )
    return jax.shard_map(
        local,
        mesh=mesh,
        in_specs=placed,
        out_specs=(P(("grp", "row"), "col"), P(("grp", "col"), "row"), P(("grp", "col"), "row")),
        check_vma=False,
    )
```

profile of v0, /device:TPU:0, one launch (start us, length us, event | category | flops | bytes accessed | tf_op | source)
XLA Modules:
  0.0 236.3 jit_solution(9814701826729110321)
XLA Ops:
  7.2 0.0 all-gather.4.cloned.1.call-start
  7.2 0.7 all-gather.4.cloned.1.call-update
  7.9 0.0 reduce-scatter.4.cloned.1.call-start
  8.0 26.9 %all-gather.4.cloned.1.call-done = bf16[512,2048]{1,0:T(8,128)(2,1)} async-done(((bf16[512,512]{1,0:T(8,128)(2,1)}), bf16[512,2048]{1,0:T(8,128)(2,1)}) %all-gather.4.cloned.1.call-update) | async-done | bytes 2097168 | tf_op jit(solution)/shard_map/all_gather | solution.py:19
  34.9 3.3 %convolution_convert_fusion = bf16[256,2048]{1,0:T(8,128)(2,1)} fusion(bf16[256,512]{1,0:T(8,128)(2,1)S(1)} %copy-done, bf16[512,2048]{1,0:T(8,128)(2,1)} %all-gather.4.cloned.1.call-done), kind=kOutput, calls=%fused_computation.3 | convolution fusion | flops 537395200 | bytes 3407872 | tf_op jit(solution)/shard_map/dot_general | solution.py:21
  38.2 0.0 all-gather.8.cloned.1.call-start
  38.2 0.7 all-gather.8.cloned.1.call-update
  38.9 0.0 all-gather.6.cloned.1.call-start
  39.0 26.5 %reduce-scatter.4.cloned.1.call-done = bf16[64,2048]{1,0:T(8,128)(2,1)} async-done(((bf16[256,2048]{1,0:T(8,128)(2,1)}), bf16[64,2048]{1,0:T(8,128)(2,1)}) %reduce-scatter.4.cloned.1.call-update) | async-done | bytes 262160 | tf_op jit(solution)/shard_map/reduce_scatter | solution.py:20
  65.5 0.0 all-reduce.2.cloned.1.call-start
  65.6 17.0 %all-gather.8.cloned.1.call-done = bf16[256,2048]{1,0:T(8,128)(2,1)} async-done(((bf16[256,512]{1,0:T(8,128)(2,1)}), bf16[256,2048]{1,0:T(8,128)(2,1)}) %all-gather.8.cloned.1.call-update) | async-done | bytes 1048592 | tf_op jit(solution)/shard_map/all_gather | solution.py:27
  82.6 29.5 %all-gather.6.cloned.1.call-done = bf16[256,2048]{1,0:T(8,128)(2,1)} async-done(((bf16[64,2048]{1,0:T(8,128)(2,1)}), bf16[256,2048]{1,0:T(8,128)(2,1)}) %all-gather.6.cloned.1.call-update) | async-done | bytes 1048592 | tf_op jit(solution)/shard_map/all_gather | solution.py:26
  112.0 2.0 fusion.8
  114.1 1.4 convolution_convert_fusion.1
  115.5 0.0 reduce-scatter.8.cloned.1.call-start
  115.6 51.4 %all-reduce.2.cloned.1.call-done = bf16[256,2048]{1,0:T(8,128)(2,1)} async-done(((bf16[256,2048]{1,0:T(8,128)(2,1)}), bf16[256,2048]{1,0:T(8,128)(2,1)}) %all-reduce.2.cloned.1.call-update) | async-done | bytes 1048592 | tf_op jit(solution)/shard_map/psum | solution.py:31
  167.0 3.3 %fusion = bf16[512,2048]{0,1:T(8,128)(2,1)} fusion(bf16[256,2048]{1,0:T(8,128)(2,1)} %all-reduce.2.cloned.1.call-done, bf16[256,512]{1,0:T(8,128)(2,1)S(1)} %copy-done), kind=kOutput, calls=%fused_computation.1 | convolution fusion | flops 538968064 | bytes 3407872 | tf_op jit(solution)/shard_map/dot_general | solution.py:11
  170.3 0.0 reduce-scatter.6.cloned.1.call-start
  170.4 1.1 copy-done.2
  171.5 1.4 fusion.1
  173.0 2.7 %fusion.2 = bf16[256,512]{1,0:T(8,128)(2,1)} fusion(bf16[256,2048]{1,0:T(8,128)(2,1)} %all-reduce.2.cloned.1.call-done, bf16[512,2048]{1,0:T(8,128)(2,1)S(1)} %copy-done.1), kind=kOutput, calls=%fused_computation.7 | convolution fusion | flops 537133056 | bytes 3407872 | tf_op jit(solution)/shard_map/dot_general | solution.py:11
  175.6 25.6 %reduce-scatter.8.cloned.1.call-done = bf16[512,512]{0,1:T(8,128)(2,1)} async-done(((bf16[512,2048]{0,1:T(8,128)(2,1)}), bf16[512,512]{0,1:T(8,128)(2,1)}) %reduce-scatter.8.cloned.1.call-update) | async-done | bytes 524304 | tf_op jit(solution)/shard_map/reduce_scatter | solution.py:36
  201.3 2.2 copy.7
  203.5 25.9 %reduce-scatter.6.cloned.1.call-done = bf16[256,512]{1,0:T(8,128)(2,1)} async-done(((bf16[256,2048]{1,0:T(8,128)(2,1)}), bf16[256,512]{1,0:T(8,128)(2,1)}) %reduce-scatter.6.cloned.1.call-update) | async-done | bytes 262160 | tf_op jit(solution)/shard_map/reduce_scatter | solution.py:39
  (14 shorter events, 0.1 us)
Async XLA Ops:
  7.2 27.7 %copy-start = (bf16[256,512]{1,0:T(8,128)(2,1)S(1)}, bf16[256,512]{1,0:T(8,128)(2,1)}, u32[]{:S(2)}) copy-start(bf16[256,512]{1,0:T(8,128)(2,1)} %param.4) | copy-start | bytes 786436
  7.2 27.7 %all-gather.4.cloned.1.call-start = ((), (), s32[]{:S(2)}) async-start(), calls=%async_computation.3 | async-start | bytes 2621440 | tf_op jit(solution)/shard_map/all_gather | solution.py:19
  7.9 104.1 %copy-start.4 = (s32[256,256]{1,0:T(8,128)S(1)}, s32[256,256]{1,0:T(8,128)}, u32[]{:S(2)}) copy-start(s32[256,256]{1,0:T(8,128)} %param.7) | copy-start | bytes 786436
  7.9 57.6 %reduce-scatter.4.cloned.1.call-start = ((), (), s32[]{:S(2)}) async-start(), calls=%async_computation.4 | async-start | bytes 1310720 | tf_op jit(solution)/shard_map/reduce_scatter | solution.py:20
  38.2 44.4 %all-gather.8.cloned.1.call-start = ((), (), s32[]{:S(2)}) async-start(), calls=%async_computation.6 | async-start | bytes 1310720 | tf_op jit(solution)/shard_map/all_gather | solution.py:27
  38.9 73.1 %all-gather.6.cloned.1.call-start = ((), (), s32[]{:S(2)}) async-start(), calls=%async_computation.5 | async-start | bytes 1310720 | tf_op jit(solution)/shard_map/all_gather | solution.py:26
  65.5 101.5 %all-reduce.2.cloned.1.call-start = ((), (), s32[]{:S(2)}) async-start(), calls=%async_computation.7 | async-start | bytes 2097152 | tf_op jit(solution)/shard_map/psum | solution.py:31
  82.5 31.5 %copy-start.3 = (bf16[256,2048]{1,0:T(8,128)(2,1)S(1)}, bf16[256,2048]{1,0:T(8,128)(2,1)}, u32[]{:S(2)}) copy-start(bf16[256,2048]{1,0:T(8,128)(2,1)} %all-gather.8.cloned.1.call-done) | copy-start | bytes 3145732
  115.5 85.7 %reduce-scatter.8.cloned.1.call-start = ((), (), s32[]{:S(2)}) async-start(), calls=%async_computation.9 | async-start | bytes 2621440 | tf_op jit(solution)/shard_map/reduce_scatter | solution.py:36
  170.3 1.2 copy-start.2
  170.3 2.7 %copy-start.1 = (bf16[512,2048]{1,0:T(8,128)(2,1)S(1)}, bf16[512,2048]{1,0:T(8,128)(2,1)}, u32[]{:S(2)}) copy-start(bf16[512,2048]{1,0:T(8,128)(2,1)} %all-gather.4.cloned.1.call-done) | copy-start | bytes 6291460
  170.3 59.1 %reduce-scatter.6.cloned.1.call-start = ((), (), s32[]{:S(2)}) async-start(), calls=%async_computation.8 | async-start | bytes 1310720 | tf_op jit(solution)/shard_map/reduce_scatter | solution.py:39
Sparse Core Ops, SparseCore 0:
  9.6 25.2 all-gather.3
  38.3 27.1 reduce-scatter.3
  67.1 15.3 all-gather.7
  84.1 27.9 all-gather.5
  115.6 51.3 all-reduce.1
  170.4 30.7 reduce-scatter.7
  204.5 24.8 reduce-scatter.5
where the time goes:
time: 237 us; the launch traced here: 236 us
  waiting for transfers between devices  204 us (86%)
  between operations  14.2 us (6%)
  matrix products  14.1 us (6%)
  local copies, waits for them, and re-layouts  3.38 us (1%)
    psum x1, waiting for transfers between devices, local(): summed = lax.psum(partial_sums.astype(jnp.bfloat16), 'col')  51.4 us
    all_gather x1, waiting for transfers between devices, local(): projected = lax.all_gather(share, 'col', axis=0, tiled=True)  29.5 us
    all_gather x1, waiting for transfers between devices, local(): w_rows = lax.all_gather(weight, 'row', axis=1, tiled=True)  26.9 us
    reduce_scatter x1, waiting for transfers between devices, local(): lax.psum_scatter(jnp.dot(programs, w_rows, preferred_element_type=jnp.flo...  26.5 us
    reduce_scatter x1, waiting for transfers between devices, local(): lax.psum_scatter(test_part.astype(jnp.bfloat16), 'row', scatter_dimension...  25.9 us
    reduce_scatter x1, waiting for transfers between devices, local(): lax.psum_scatter(weight_part.astype(jnp.bfloat16), 'row', scatter_dimensi...  25.6 us
    all_gather x1, waiting for transfers between devices, local(): test_whole = lax.all_gather(tests, 'row', axis=1, tiled=True)  17 us
    dot_general x4, matrix products, contract(): lax.dot_general(left, right, (((left_dim,), (right_dim,)), ((), ())), pre...  9.44 us
  transfers between devices with their start and end apart: 7, of which 7 were waited for; matrix products, arithmetic and copies ran while one was open for 3% of the time, Pallas kernels for 0%

commit v1 on v0

--- a/solution.py
+++ b/solution.py
@@ -23,7 +23,16 @@
         scatter_dimension=0,
         tiled=True,
     )
-    projected = lax.all_gather(share, "col", axis=0, tiled=True)
+    axis_n = jax.lax.axis_size("col")
+    before = [(idx - 1, idx) for idx in range(1, axis_n)] + [(axis_n - 1, 0)]
+    found_now = share
+    pile = [found_now]
+    for _ in tuple(range(axis_n - 1)):
+        found_now = jax.lax.ppermute(found_now, "col", before)
+        pile += [found_now]
+    tile_out = jnp.concatenate([*reversed(pile)], axis=0)
+    local_part = jax.lax.axis_index("col")
+    projected = jnp.roll(tile_out, shift=(local_part + 1) * found_now.shape[0], axis=0)
     test_whole = lax.all_gather(tests, "row", axis=1, tiled=True)
     logits = contract(projected, test_whole, 1, 1) * factor
     dlogits = (jax.nn.sigmoid(logits) - targets).astype(jnp.bfloat16)

time: 237 us -> 227 us (0.958)
  waiting for transfers between devices: 204 us -> 195 us
    all_gather x1 -> x0, waiting for transfers between devices: 29.5 us -> none  [local(): projected = lax.all_gather(share, 'col', axis=0, tiled=True)]
    ppermute x0 -> x3, waiting for transfers between devices: none -> 26.8 us  [local(): found_now = jax.lax.ppermute(found_now, 'col', before)]
    all_gather x1, waiting for transfers between devices: 17 us -> 8.91 us  [local(): test_whole = lax.all_gather(tests, 'row', axis=1, tiled=True)]
  transfers between devices with their start and end apart: 7 -> 9, of which waited for: 7 -> 9; matrix products, arithmetic and copies ran while one was open for 3% -> 3% of each run, Pallas kernels for 0% -> 0%
where the time goes in v1:
time: 227 us
  waiting for transfers between devices  195 us (86%)
  between operations  14.3 us (6%)
  matrix products  14.2 us (6%)
  local copies, waits for them, and re-layouts  3.36 us (1%)
    psum x1, waiting for transfers between devices, local(): summed = lax.psum(partial_sums.astype(jnp.bfloat16), 'col')  51.9 us
    reduce_scatter x1, waiting for transfers between devices, local(): lax.psum_scatter(jnp.dot(programs, w_rows, preferred_element_type=jnp.flo...  27.2 us
    all_gather x1, waiting for transfers between devices, local(): w_rows = lax.all_gather(weight, 'row', axis=1, tiled=True)  26.9 us
    ppermute x3, waiting for transfers between devices, local(): found_now = jax.lax.ppermute(found_now, 'col', before)  26.8 us
    reduce_scatter x1, waiting for transfers between devices, local(): lax.psum_scatter(weight_part.astype(jnp.bfloat16), 'row', scatter_dimensi...  26.5 us
    reduce_scatter x1, waiting for transfers between devices, local(): lax.psum_scatter(test_part.astype(jnp.bfloat16), 'row', scatter_dimension...  25.8 us
    dot_general x4, matrix products, contract(): lax.dot_general(left, right, (((left_dim,), (right_dim,)), ((), ())), pre...  9.46 us
    all_gather x1, waiting for transfers between devices, local(): test_whole = lax.all_gather(tests, 'row', axis=1, tiled=True)  8.91 us
  transfers between devices with their start and end apart: 9, of which 9 were waited for; matrix products, arithmetic and copies ran while one was open for 3% of the time, Pallas kernels for 0%

profile of v1, /device:TPU:0, one launch (start us, length us, event | category | flops | bytes accessed | tf_op | source)
XLA Modules:
  0.0 226.9 jit_solution(1429538750219710598)
XLA Ops:
  7.2 0.0 all-gather.3.cloned.1.call-start
  7.2 0.7 all-gather.3.cloned.1.call-update
  7.9 0.0 reduce-scatter.4.cloned.1.call-start
  8.0 26.9 %all-gather.3.cloned.1.call-done = bf16[512,2048]{1,0:T(8,128)(2,1)} async-done(((bf16[512,512]{1,0:T(8,128)(2,1)}), bf16[512,2048]{1,0:T(8,128)(2,1)}) %all-gather.3.cloned.1.call-update) | async-done | bytes 2097168 | tf_op jit(solution)/shard_map/all_gather | solution.py:19
  34.9 3.3 %convolution_convert_fusion = bf16[256,2048]{1,0:T(8,128)(2,1)} fusion(bf16[256,512]{1,0:T(8,128)(2,1)S(1)} %copy-done, bf16[512,2048]{1,0:T(8,128)(2,1)} %all-gather.3.cloned.1.call-done), kind=kOutput, calls=%fused_computation.3 | convolution fusion | flops 537395200 | bytes 3407872 | tf_op jit(solution)/shard_map/dot_general | solution.py:21
  38.2 0.0 all-gather.5.cloned.1.call-start
  38.2 27.2 %reduce-scatter.4.cloned.1.call-done = bf16[64,2048]{1,0:T(8,128)(2,1)} async-done(((bf16[256,2048]{1,0:T(8,128)(2,1)}), bf16[64,2048]{1,0:T(8,128)(2,1)}) %reduce-scatter.4.cloned.1.call-update) | async-done | bytes 262160 | tf_op jit(solution)/shard_map/reduce_scatter | solution.py:20
  65.5 9.9 %collective-permute-done = bf16[64,2048]{1,0:T(8,128)(2,1)S(1)} collective-permute-done((bf16[64,2048]{1,0:T(8,128)(2,1)}, bf16[64,2048]{1,0:T(8,128)(2,1)S(1)}, u32[]{:S(2)}, u32[]{:S(2)}) %collective-permute-start) | collective-permute-done | bytes 262176 | tf_op jit(solution)/shard_map/ppermute | solution.py:31
  75.4 8.8 %collective-permute-done.1 = bf16[64,2048]{1,0:T(8,128)(2,1)S(1)} collective-permute-done((bf16[64,2048]{1,0:T(8,128)(2,1)S(1)}, bf16[64,2048]{1,0:T(8,128)(2,1)S(1)}, u32[]{:S(2)}, u32[]{:S(2)}) %collective-permute-start.1) | collective-permute-done | bytes 262176 | tf_op jit(solution)/shard_map/ppermute | solution.py:31
  84.2 0.0 all-reduce.2.cloned.1.call-start
  84.3 8.1 %collective-permute-done.2 = bf16[64,2048]{1,0:T(8,128)(2,1)S(1)} collective-permute-done((bf16[64,2048]{1,0:T(8,128)(2,1)S(1)}, bf16[64,2048]{1,0:T(8,128)(2,1)S(1)}, u32[]{:S(2)}, u32[]{:S(2)}) %collective-permute-start.2) | collective-permute-done | bytes 262176 | tf_op jit(solution)/shard_map/ppermute | solution.py:31
  92.4 1.0 constant_dynamic-update-slice_fusion.4
  93.5 8.9 %all-gather.5.cloned.1.call-done = bf16[256,2048]{1,0:T(8,128)(2,1)} async-done(((bf16[256,512]{1,0:T(8,128)(2,1)}), bf16[256,2048]{1,0:T(8,128)(2,1)}) %all-gather.5.cloned.1.call-update) | async-done | bytes 1048592 | tf_op jit(solution)/shard_map/all_gather | solution.py:36
  102.4 1.8 fusion.8
  104.3 1.4 convolution_convert_fusion.1
  105.7 0.0 reduce-scatter.8.cloned.1.call-start
  105.8 51.9 %all-reduce.2.cloned.1.call-done = bf16[256,2048]{1,0:T(8,128)(2,1)} async-done(((bf16[256,2048]{1,0:T(8,128)(2,1)}), bf16[256,2048]{1,0:T(8,128)(2,1)}) %all-reduce.2.cloned.1.call-update) | async-done | bytes 1048592 | tf_op jit(solution)/shard_map/psum | solution.py:40
  157.7 3.3 %fusion = bf16[512,2048]{0,1:T(8,128)(2,1)} fusion(bf16[256,2048]{1,0:T(8,128)(2,1)} %all-reduce.2.cloned.1.call-done, bf16[256,512]{1,0:T(8,128)(2,1)S(1)} %copy-done), kind=kOutput, calls=%fused_computation.1 | convolution fusion | flops 538968064 | bytes 3407872 | tf_op jit(solution)/shard_map/dot_general | solution.py:11
  161.1 0.0 reduce-scatter.6.cloned.1.call-start
  161.1 2.9 %fusion.1 = bf16[256,2048]{1,0:T(8,128)(2,1)} fusion(bf16[256,256]{1,0:T(8,128)(2,1)S(1)} %fusion.8, bf16[512,2048]{1,0:T(8,128)(2,1)} %copy-done.4, s32[]{:T(128)S(6)} %select_n.14), kind=kOutput, calls=%fused_computation.4 | convolution fusion | flops 269484032 | bytes 2228228 | tf_op jit(solution)/shard_map/dot_general | solution.py:11
  164.0 1.5 fusion.2
  165.5 26.5 %reduce-scatter.8.cloned.1.call-done = bf16[512,512]{0,1:T(8,128)(2,1)} async-done(((bf16[512,2048]{0,1:T(8,128)(2,1)}), bf16[512,512]{0,1:T(8,128)(2,1)}) %reduce-scatter.8.cloned.1.call-update) | async-done | bytes 524304 | tf_op jit(solution)/shard_map/reduce_scatter | solution.py:45
  192.0 2.2 copy.7
  194.2 25.8 %reduce-scatter.6.cloned.1.call-done = bf16[256,512]{1,0:T(8,128)(2,1)} async-done(((bf16[256,2048]{1,0:T(8,128)(2,1)}), bf16[256,512]{1,0:T(8,128)(2,1)}) %reduce-scatter.6.cloned.1.call-update) | async-done | bytes 262160 | tf_op jit(solution)/shard_map/reduce_scatter | solution.py:48
  (27 shorter events, 0.3 us)
Async XLA Ops:
  7.2 27.7 %copy-start = (bf16[256,512]{1,0:T(8,128)(2,1)S(1)}, bf16[256,512]{1,0:T(8,128)(2,1)}, u32[]{:S(2)}) copy-start(bf16[256,512]{1,0:T(8,128)(2,1)} %param.4) | copy-start | bytes 786436
  7.2 27.7 %all-gather.3.cloned.1.call-start = ((), (), s32[]{:S(2)}) async-start(), calls=%async_computation.3 | async-start | bytes 2621440 | tf_op jit(solution)/shard_map/all_gather | solution.py:19
  7.9 57.6 %reduce-scatter.4.cloned.1.call-start = ((), (), s32[]{:S(2)}) async-start(), calls=%async_computation.4 | async-start | bytes 1310720 | tf_op jit(solution)/shard_map/reduce_scatter | solution.py:20
  38.2 64.2 %all-gather.5.cloned.1.call-start = ((), (), s32[]{:S(2)}) async-start(), calls=%async_computation.5 | async-start | bytes 1310720 | tf_op jit(solution)/shard_map/all_gather | solution.py:36
  65.5 28.0 %copy-start.3 = (bf16[64,2048]{1,0:T(8,128)(2,1)S(1)}, bf16[64,2048]{1,0:T(8,128)(2,1)}, u32[]{:S(2)}) copy-start(bf16[64,2048]{1,0:T(8,128)(2,1)} %reduce-scatter.4.cloned.1.call-done) | copy-start | bytes 786436
  65.5 9.9 %collective-permute-start = (bf16[64,2048]{1,0:T(8,128)(2,1)}, bf16[64,2048]{1,0:T(8,128)(2,1)S(1)}, u32[]{:S(2)}, u32[]{:S(2)}) collective-permute-start(bf16[64,2048]{1,0:T(8,128)(2,1)} %reduce-scatter.4.cloned.1.call-done), channel_id=1, source_target_pairs={{0,1},{1,2},{2,3},{3,0},{4,5},{5,6},{6,7},{7,4},{8,9},{9,10},{10,1... | collective-permute-start | bytes 786440 | tf_op jit(solution)/shard_map/ppermute | solution.py:31
  75.4 8.8 %collective-permute-start.1 = (bf16[64,2048]{1,0:T(8,128)(2,1)S(1)}, bf16[64,2048]{1,0:T(8,128)(2,1)S(1)}, u32[]{:S(2)}, u32[]{:S(2)}) collective-permute-start(bf16[64,2048]{1,0:T(8,128)(2,1)S(1)} %collective-permute-done), channel_id=1, source_target_pairs={{0,1},{1,2},{2,3},{3,0},{4,5},{5,6},{6,7},{7,4},{8,9},{9,10},{10,1... | collective-permute-start | bytes 786440 | tf_op jit(solution)/shard_map/ppermute | solution.py:31
  84.2 8.2 %collective-permute-start.2 = (bf16[64,2048]{1,0:T(8,128)(2,1)S(1)}, bf16[64,2048]{1,0:T(8,128)(2,1)S(1)}, u32[]{:S(2)}, u32[]{:S(2)}) collective-permute-start(bf16[64,2048]{1,0:T(8,128)(2,1)S(1)} %collective-permute-done.1), channel_id=1, source_target_pairs={{0,1},{1,2},{2,3},{3,0},{4,5},{5,6},{6,7},{7,4},{8,9},{9,10},{10,1... | collective-permute-start | bytes 786440 | tf_op jit(solution)/shard_map/ppermute | solution.py:31
  84.2 73.5 %all-reduce.2.cloned.1.call-start = ((), (), s32[]{:S(2)}) async-start(), calls=%async_computation.6 | async-start | bytes 2097152 | tf_op jit(solution)/shard_map/psum | solution.py:40
  93.5 12.2 %copy-start.4 = (bf16[512,2048]{1,0:T(8,128)(2,1)}, bf16[512,2048]{1,0:T(8,128)(2,1)S(1)}, u32[]{:S(2)}) copy-start(bf16[512,2048]{1,0:T(8,128)(2,1)S(1)} %constant_dynamic-update-slice_fusion) | copy-start | bytes 6291460
  102.4 1.9 copy-start.2
  105.7 86.3 %reduce-scatter.8.cloned.1.call-start = ((), (), s32[]{:S(2)}) async-start(), calls=%async_computation.8 | async-start | bytes 2621440 | tf_op jit(solution)/shard_map/reduce_scatter | solution.py:45
  161.1 3.0 %copy-start.1 = (bf16[512,2048]{1,0:T(8,128)(2,1)S(1)}, bf16[512,2048]{1,0:T(8,128)(2,1)}, u32[]{:S(2)}) copy-start(bf16[512,2048]{1,0:T(8,128)(2,1)} %all-gather.3.cloned.1.call-done) | copy-start | bytes 6291460
  161.1 3.0 %copy-start.5 = (bf16[256,2048]{1,0:T(8,128)(2,1)S(1)}, bf16[256,2048]{1,0:T(8,128)(2,1)}, u32[]{:S(2)}) copy-start(bf16[256,2048]{1,0:T(8,128)(2,1)} %all-reduce.2.cloned.1.call-done) | copy-start | bytes 3145732
  161.1 59.0 %reduce-scatter.6.cloned.1.call-start = ((), (), s32[]{:S(2)}) async-start(), calls=%async_computation.7 | async-start | bytes 1310720 | tf_op jit(solution)/shard_map/reduce_scatter | solution.py:48
Sparse Core Ops, SparseCore 0:
  9.6 25.2 all-gather.2
  38.3 27.1 reduce-scatter.3
  84.3 18.0 all-gather.4
  105.9 51.8 all-reduce.1
  161.2 30.7 reduce-scatter.7
  195.1 24.8 reduce-scatter.5
